TPU v7x, 256 devices: a whole 4x4x8 slice. The times are simulated.
256 devices in a mesh: seq: 32 (over y, x, core), tp: 8 (over z).
Axes of the slice: x: 4, y: 4, z: 8, core: 2. Of those that a mesh axis runs over, the one named last changes fastest.
Arguments:
- tokens: bfloat16 [8192, 4096], P('seq', 'tp'), may hold values from -11 to 11
- grad_out: bfloat16 [8192, 4096], P('seq', 'tp'), may hold values from -1.5 to 1.5
- in_weight: bfloat16 [4096, 4096], P('seq', 'tp'), may hold values from -0.09880682 to 0.09880682
- in_scale: float32 [4096], P('tp'), may hold values from 0.0008238636 to 0.010511364
- out_weight: bfloat16 [4096, 4096], P('seq', 'tp'), may hold values from -0.053943182 to 0.053943182
- out_scale: float32 [4096], replicated, may hold values from 0.00139204545 to 0.0057386364
- state_in: bfloat16 [8192, 128], P('seq'), may hold values from -0.0625 to 0.0625
- state_out: bfloat16 [8192, 128], P('seq'), may hold values from -6 to 6
- log_decay: float32 [8192, 64], P('seq', 'tp'), may hold values from -1.6 to 0
Outputs:
- grad_tokens: bfloat16 [8192, 4096], P('seq', 'tp')
- grad_in_weight: float32 [4096, 4096], P('seq', 'tp')
- grad_in_scale: float32 [4096], P('tp')
- grad_out_weight: float32 [4096, 4096], P('seq', 'tp')
- grad_out_scale: float32 [4096], P('seq')
All inputs are finite; a program needn't handle non-finite values.
Results may differ from a plain program's by a relative error of at most 0.027.
Values may be sent and summed in bfloat16 or wider, within the bound.
No kernel may reach another device: no remote copies, remote signals or barrier semaphores. Data moves between devices by JAX's collectives and lax.ppermute only.
A program may use at most 128 MiB of HBM per device.

v0:
```python
import jax
import jax.numpy as jnp
from jax import lax
from jax.sharding import PartitionSpec as P

D = 4096
HEADS = 64
HEAD_DIM = 64
STRETCH = 256
QMAX = 7
precise = lax.Precision.HIGHEST


def prefix(array, axis, join, neutral, backward):
    count = lax.axis_size(axis)
    place = lax.axis_index(axis)
    ahead = count - 1 - place if backward else place
    gathered = jax.tree.map(
        lambda a, kind: lax.all_gather(a.astype(kind), axis), array, (jnp.bfloat16, jnp.bfloat16)
    )
    state = jax.tree.map(lambda a, e: jnp.zeros_like(a) + jnp.asarray(e, a.dtype), array, neutral)

    def one(turn, state):
        source = count - 1 - turn if backward else turn
        return join(
            state,
            jax.tree.map(
                lambda a, own: lax.dynamic_index_in_dim(a, source, 0, False).astype(own.dtype),
                gathered,
                array,
            ),
        )

    return lax.fori_loop(0, ahead, one, state)


def quantize(weight, channel_scale):
    ratios = weight.astype(jnp.float32) / channel_scale
    clipped = jnp.clip(ratios, -QMAX, QMAX)
    levels = jnp.floor(clipped + 0.5)
    inside = jnp.abs(ratios) <= QMAX
    slopes = jnp.where(inside, levels - ratios, levels)
    return (levels, slopes, inside.astype(jnp.float32))


def stretch_terms(decay_logs, inputs_f, outputs_f):
    cumul = jnp.cumsum(decay_logs, axis=0)
    ending = cumul[-1]
    spread = cumul[:, None, :] - cumul[None, :, :]
    length = decay_logs.shape[0]
    causal = jnp.arange(length)[:, None] >= jnp.arange(length)[None, :]
    mixing = jnp.exp(jnp.where(causal[:, :, None], spread, -jnp.inf))
    intersection = jnp.dot(outputs_f, inputs_f.T, precision=precise)
    return (cumul, ending, mixing * intersection[:, :, None])


def forward_step(carried, pieces):
    values, cumul, ending, weights, inputs_f, outputs_f = pieces
    inner = jnp.einsum("sth,thp->shp", weights, values, precision=precise)
    outer = jnp.exp(cumul)[:, :, None] * jnp.einsum(
        "sn,hnp->shp", outputs_f, carried, precision=precise
    )
    fresh = jnp.einsum(
        "th,tn,thp->hnp", jnp.exp(ending[None, :] - cumul), inputs_f, values, precision=precise
    )
    return (jnp.exp(ending)[:, None, None] * carried + fresh, inner + outer)


def backward_step(carried, pieces):
    grads, cumul, ending, weights, inputs_f, outputs_f = pieces
    inner = jnp.einsum("sth,shp->thp", weights, grads, precision=precise)
    outer = jnp.exp(ending[None, :] - cumul)[:, :, None] * jnp.einsum(
        "tn,hnp->thp", inputs_f, carried, precision=precise
    )
    fresh = jnp.einsum("sh,sn,shp->hnp", jnp.exp(cumul), outputs_f, grads, precision=precise)
    return (jnp.exp(ending)[:, None, None] * carried + fresh, inner + outer)


def join_forward(earlier, later):
    return (earlier[0] * later[0], later[0][:, None, None] * earlier[1] + later[1])


def join_backward(earlier, later):
    return (earlier[0] * later[0], later[1] + later[0][:, None, None] * earlier[1])


def per_device(
    tokens, grad_out, in_weight, in_scale, out_weight, out_scale, state_in, state_out, log_decay
):
    local_rows = tokens.shape[0]
    heads_here = log_decay.shape[1]
    width_here = in_scale.shape[0]
    head_size = width_here // heads_here
    state_size = state_in.shape[1]
    weight_rows = in_weight.shape[0]
    blocks = local_rows // STRETCH
    row_start = lax.axis_index("seq") * weight_rows
    out_scale_rows = lax.dynamic_slice_in_dim(out_scale, row_start, weight_rows)
    in_levels, in_slopes, in_inside = quantize(in_weight, in_scale[None, :])
    out_levels, out_slopes, out_inside = quantize(out_weight, out_scale_rows[:, None])
    in_codes = lax.all_gather(in_levels.astype(jnp.bfloat16), "seq", axis=0, tiled=True)
    out_codes = lax.all_gather(out_levels.astype(jnp.bfloat16), "seq", axis=0, tiled=True)
    features = lax.all_gather(tokens, "tp", axis=1, tiled=True)
    cotangent = lax.all_gather(grad_out, "tp", axis=1, tiled=True)
    projected = jnp.dot(features, in_codes, preferred_element_type=jnp.float32) * in_scale[None, :]
    scaled_grad = (cotangent.astype(jnp.float32) * out_scale[None, :]).astype(jnp.bfloat16)
    grad_mixed = jnp.dot(scaled_grad, out_codes, preferred_element_type=jnp.float32)
    inputs_full = state_in.astype(jnp.float32)
    outputs_full = state_out.astype(jnp.float32)
    decay_blocks = log_decay.reshape(blocks, STRETCH, heads_here)
    input_blocks = inputs_full.reshape(blocks, STRETCH, state_size)
    output_blocks = outputs_full.reshape(blocks, STRETCH, state_size)
    cumul, ending, weights = jax.vmap(stretch_terms)(decay_blocks, input_blocks, output_blocks)
    value_blocks = projected.reshape(blocks, STRETCH, heads_here, head_size)
    grad_blocks = grad_mixed.reshape(blocks, STRETCH, heads_here, head_size)
    empty = jnp.zeros((heads_here, state_size, head_size), jnp.float32)
    local_state, mixed_local = lax.scan(
        forward_step, empty, (value_blocks, cumul, ending, weights, input_blocks, output_blocks)
    )
    local_grad_state, grad_local = lax.scan(
        backward_step,
        empty,
        (grad_blocks, cumul, ending, weights, input_blocks, output_blocks),
        reverse=True,
    )
    running = jnp.cumsum(log_decay, axis=0)
    device_total = running[-1]
    device_decay = jnp.exp(device_total)
    identity = (jnp.ones_like(device_decay), empty)
    entering = prefix((device_decay, local_state), "seq", join_forward, identity, False)[1]
    leaving = prefix((device_decay, local_grad_state), "seq", join_backward, identity, True)[1]
    mixed = mixed_local.reshape(local_rows, heads_here, head_size) + jnp.exp(running)[
        :, :, None
    ] * jnp.einsum("tn,hnp->thp", outputs_full, entering, precision=precise)
    grad_values = grad_local.reshape(local_rows, heads_here, head_size) + jnp.exp(
        device_total[None, :] - running
    )[:, :, None] * jnp.einsum("tn,hnp->thp", inputs_full, leaving, precision=precise)
    mixed = mixed.reshape(local_rows, width_here)
    grad_values = grad_values.reshape(local_rows, width_here)
    mixed_b = mixed.astype(jnp.bfloat16)
    grad_b = grad_values.astype(jnp.bfloat16)
    grad_scaled = (grad_values * in_scale[None, :]).astype(jnp.bfloat16)
    piece = features
    in_total = lax.psum_scatter(
        jnp.einsum("td,tc->dc", piece, grad_b, preferred_element_type=jnp.float32).astype(
            jnp.bfloat16
        ),
        "seq",
        scatter_dimension=0,
        tiled=True,
    ).astype(jnp.float32)
    piece = cotangent
    out_total = lax.psum_scatter(
        jnp.einsum("td,tc->dc", piece, mixed_b, preferred_element_type=jnp.float32).astype(
            jnp.bfloat16
        ),
        "seq",
        scatter_dimension=0,
        tiled=True,
    ).astype(jnp.float32)
    partial_tokens = jnp.einsum(
        "tc,dc->td", grad_scaled, in_codes, preferred_element_type=jnp.float32
    )
    grad_tokens = lax.psum_scatter(
        partial_tokens.astype(jnp.bfloat16), "tp", scatter_dimension=1, tiled=True
    )
    in_part = jnp.sum(in_total * in_slopes, axis=0)
    out_part = jnp.sum(out_total * out_slopes, axis=1)
    in_sum = lax.psum(in_part, "seq")
    out_sum = lax.psum(out_part, "tp")
    grad_in_scale = in_sum / jnp.sqrt(jnp.float32(D * QMAX))
    grad_out_scale = out_sum / jnp.sqrt(jnp.float32(HEADS * HEAD_DIM * QMAX))
    return (
        grad_tokens,
        in_total * in_inside,
        grad_in_scale,
        out_total * out_inside,
        grad_out_scale,
    )


def solution(mesh):
    placed = (
        P("seq", "tp"),
        P("seq", "tp"),
        P("seq", "tp"),
        P("tp"),
        P("seq", "tp"),
        P(),
        P("seq", None),
        P("seq", None),
        P("seq", "tp"),
    )
    return jax.shard_map(
        per_device,
        mesh=mesh,
        in_specs=placed,
        out_specs=(P("seq", "tp"), P("seq", "tp"), P("tp"), P("seq", "tp"), P("seq")),
        check_vma=False,
    )
```

profile of v0, /device:TPU:6, one launch (start us, length us, event | category | flops | bytes accessed | tf_op | source)
XLA Modules:
  0.0 612.6 jit_solution(15400213899961906926)
XLA Ops:
  8.0 1.0 copy.60
  10.5 1.3 reduce-window.14
  12.4 41.5 %all-gather.10.cloned.1.call-done = bf16[256,4096]{1,0:T(8,128)(2,1)} async-done(((bf16[256,512]{1,0:T(8,128)(2,1)}), bf16[256,4096]{1,0:T(8,128)(2,1)}) %all-gather.10.cloned.1.call-update) | async-done | bytes 2097168 | tf_op jit(solution)/shard_map/all_gather | solution.py:104
  53.9 55.4 %all-gather.12.cloned.1.call-done = bf16[4096,512]{0,1:T(8,128)(2,1)} async-done(((bf16[128,512]{0,1:T(8,128)(2,1)}), bf16[4096,512]{0,1:T(8,128)(2,1)}) %all-gather.12.cloned.1.call-update) | async-done | bytes 4194320 | tf_op jit(solution)/shard_map/all_gather | solution.py:102
  109.3 4.1 fusion.2
  113.4 1.0 fusion.20
  116.2 18.9 %all-gather.2 = bf16[32,1,8]{2,1,0:T(2,128)(2,1)S(1)} all-gather(bf16[1,1,8]{2,1,0:T(2,128)(2,1)S(1)} %bitcast.154), channel_id=1, replica_groups=mesh['seq'=32,'tp'=8] {'seq'}, dimensions={0}, use_global_device_ids=true | all-gather | bytes 528 | tf_op jit(solution)/shard_map/all_gather | solution.py:19
  135.6 1.8 fusion.6
  137.5 28.1 %all-gather.18.cloned.1.call-done = bf16[256,128,64]{1,2,0:T(8,128)(2,1)} async-done(((bf16[8,128,64]{1,2,0:T(8,128)(2,1)}), bf16[256,128,64]{1,2,0:T(8,128)(2,1)}) %all-gather.18.cloned.1.call-update) | async-done | bytes 4194320 | tf_op jit(solution)/shard_map/all_gather | solution.py:19
  165.6 32.6 %while.16 = (s32[]{:T(128)}, f32[8,128,64]{2,1,0:T(8,128)S(1)}, s32[]{:T(128)}, bf16[32,8,128,64]{2,3,1,0:T(8,128)(2,1)}, bf16[32,8]{1,0:T(8,128)(2,1)S(1)}, /*index=5*/s32[]{:T(128)}, s32[]{:T(128)}, s32[]{:T(128)}, s32[]{:T(128)}) while((s32[]{:T(128)}, f32[8,128,64]{2,1,0:T(8,128)S(1)}, s32[]{:T(128)}, bf16[32,8,128,64]{2,3,1,0:T(8,128)(2,1)}, ...), condition=%wide.region_5.6_spmd, body=%wide.region_4.5_spmd.sunk | while | flops 196622 | bytes 1179883 | solution.py:34
  165.6 0.9 constant_dynamic-slice_fusion.4
  166.9 0.9 constant_dynamic-slice_fusion.4
  168.2 0.9 constant_dynamic-slice_fusion.4
  169.5 0.9 constant_dynamic-slice_fusion.4
  170.8 0.9 constant_dynamic-slice_fusion.4
  172.1 0.9 constant_dynamic-slice_fusion.4
  173.4 0.9 constant_dynamic-slice_fusion.4
  174.7 0.9 constant_dynamic-slice_fusion.4
  176.0 0.9 constant_dynamic-slice_fusion.4
  177.3 0.9 constant_dynamic-slice_fusion.4
  178.6 0.9 constant_dynamic-slice_fusion.4
  179.9 0.9 constant_dynamic-slice_fusion.4
  181.3 0.9 constant_dynamic-slice_fusion.4
  182.6 0.9 constant_dynamic-slice_fusion.4
  183.9 0.9 constant_dynamic-slice_fusion.4
  185.2 0.9 constant_dynamic-slice_fusion.4
  186.5 0.9 constant_dynamic-slice_fusion.4
  187.8 0.9 constant_dynamic-slice_fusion.4
  189.1 0.9 constant_dynamic-slice_fusion.4
  190.4 0.9 constant_dynamic-slice_fusion.4
  191.7 0.9 constant_dynamic-slice_fusion.4
  193.0 0.9 constant_dynamic-slice_fusion.4
  194.3 0.9 constant_dynamic-slice_fusion.4
  195.6 0.9 constant_dynamic-slice_fusion.4
  196.9 0.9 constant_dynamic-slice_fusion.4
  199.3 8.6 %all-gather.16.cloned.1.call-done = bf16[256,4096]{1,0:T(8,128)(2,1)} async-done(((bf16[256,512]{1,0:T(8,128)(2,1)}), bf16[256,4096]{1,0:T(8,128)(2,1)}) %all-gather.16.cloned.1.call-update) | async-done | bytes 2097168 | tf_op jit(solution)/shard_map/all_gather | solution.py:103
  207.9 4.8 fusion
  212.7 6.5 %copy.81 = bf16[4096,512]{1,0:T(8,128)(2,1)} copy(bf16[4096,512]{0,1:T(8,128)(2,1)} %fusion) | data formatting | bytes 8388608
  219.2 0.8 copy-done.7
  220.2 87.2 %reduce-scatter.10.cloned.1.call-done = bf16[128,512]{1,0:T(8,128)(2,1)} async-done(((bf16[4096,512]{1,0:T(8,128)(2,1)}), bf16[128,512]{1,0:T(8,128)(2,1)}) %reduce-scatter.10.cloned.1.call-update) | async-done | bytes 131088
  307.4 1.0 copy.82
  308.4 0.9 fusion.34
  309.3 54.8 %all-gather.14.cloned.1.call-done = bf16[4096,512]{0,1:T(8,128)(2,1)} async-done(((bf16[128,512]{0,1:T(8,128)(2,1)}), bf16[4096,512]{0,1:T(8,128)(2,1)}) %all-gather.14.cloned.1.call-update) | async-done | bytes 4194320 | tf_op jit(solution)/shard_map/all_gather | solution.py:101
  364.1 3.5 convolution_multiply_fusion
  368.4 1.0 fusion.19
  369.6 3.5 fusion.7
  373.0 47.4 %all-gather.20.cloned.1.call-done = bf16[256,128,64]{1,2,0:T(8,128)(2,1)} async-done(((bf16[8,128,64]{1,2,0:T(8,128)(2,1)}), bf16[256,128,64]{1,2,0:T(8,128)(2,1)}) %all-gather.20.cloned.1.call-update) | async-done | bytes 4194320 | tf_op jit(solution)/shard_map/all_gather | solution.py:19
  420.5 8.0 %while.17 = (s32[]{:T(128)}, f32[8,128,64]{2,1,0:T(8,128)S(1)}, s32[]{:T(128)}, bf16[32,8]{1,0:T(8,128)(2,1)S(1)}, bf16[32,8,128,64]{2,3,1,0:T(8,128)(2,1)}, /*index=5*/s32[]{:T(128)}, s32[]{:T(128)}, s32[]{:T(128)}) while((s32[]{:T(128)}, f32[8,128,64]{2,1,0:T(8,128)S(1)}, s32[]{:T(128)}, bf16[32,8]{1,0:T(8,128)(2,1)S(1)}, ...), condition=%wide.region_11.12_spmd, body=%wide.region_10.11_spmd.sunk | while | flops 196621 | bytes 1179863 | solution.py:34
  420.5 0.9 constant_dynamic-slice_fusion.5
  421.8 0.9 constant_dynamic-slice_fusion.5
  423.1 0.9 constant_dynamic-slice_fusion.5
  424.4 0.9 constant_dynamic-slice_fusion.5
  425.7 0.9 constant_dynamic-slice_fusion.5
  427.1 0.9 constant_dynamic-slice_fusion.5
  430.1 3.2 fusion.1
  433.4 6.5 %copy.83 = bf16[4096,512]{1,0:T(8,128)(2,1)} copy(bf16[4096,512]{0,1:T(8,128)(2,1)} %fusion.1) | data formatting | bytes 8388608
  440.1 4.9 convolution_convert_fusion.2
  445.0 0.8 copy.72
  445.8 83.4 %psum.14 = f32[512]{0:T(512)S(1)} all-reduce(f32[512]{0:T(512)S(1)} %get-tuple-element.273), channel_id=1, replica_groups=mesh['seq'=32,'tp'=8] {'seq'}, use_global_device_ids=true, to_apply=%region_9.10 | all-reduce | flops 512 | bytes 4096 | tf_op jit(solution)/shard_map/psum | solution.py:169
  529.8 31.0 %reduce-scatter.12.cloned.1.call-done = bf16[128,512]{1,0:T(8,128)(2,1)} async-done(((bf16[4096,512]{1,0:T(8,128)(2,1)}), bf16[128,512]{1,0:T(8,128)(2,1)}) %reduce-scatter.12.cloned.1.call-update) | async-done | bytes 131088
  560.8 1.0 copy.84
  562.0 0.8 copy.73
  562.8 17.4 %psum.15 = f32[128]{0:T(128)S(1)} all-reduce(f32[128]{0:T(128)S(1)} %get-tuple-element.275), channel_id=1, replica_groups=mesh['seq'=32,'tp'=8] {'tp'}, use_global_device_ids=true, to_apply=%region_14.15 | all-reduce | flops 128 | bytes 1024 | tf_op jit(solution)/shard_map/psum | solution.py:170
  580.7 25.3 %reduce-scatter.8.cloned.1.call-done = bf16[256,512]{1,0:T(8,128)(2,1)} async-done(((bf16[256,4096]{1,0:T(8,128)(2,1)}), bf16[256,512]{1,0:T(8,128)(2,1)}) %reduce-scatter.8.cloned.1.call-update) | async-done | bytes 262160 | tf_op jit(solution)/shard_map/reduce_scatter | solution.py:164
  (163 shorter events, 21.0 us)
Async XLA Ops:
  7.2 128.3 %copy-start = (bf16[256,128]{1,0:T(8,128)(2,1)S(1)}, bf16[256,128]{1,0:T(8,128)(2,1)}, u32[]{:S(2)}) copy-start(bf16[256,128]{1,0:T(8,128)(2,1)} %param.19) | copy-start | bytes 196612
  7.2 46.7 %all-gather.10.cloned.1.call-start = ((), (), s32[]{:S(2)}) async-start(), calls=%async_computation.3 | async-start | bytes 2359296 | tf_op jit(solution)/shard_map/all_gather | solution.py:104
  7.9 101.4 %all-gather.12.cloned.1.call-start = ((), (), s32[]{:S(2)}) async-start(), calls=%async_computation.4 | async-start | bytes 4325376 | tf_op jit(solution)/shard_map/all_gather | solution.py:102
  10.5 155.0 %all-gather.18.cloned.1.call-start = ((), (), s32[]{:S(2)}) async-start(), calls=%async_computation.8 | async-start | bytes 4325376 | tf_op jit(solution)/shard_map/all_gather | solution.py:19
  12.4 101.1 %copy-start.3 = (bf16[256,128]{1,0:T(8,128)(2,1)S(1)}, bf16[256,128]{1,0:T(8,128)(2,1)}, u32[]{:S(2)}) copy-start(bf16[256,128]{1,0:T(8,128)(2,1)} %param.20) | copy-start | bytes 196612
  12.4 102.8 %copy-start.8 = (f32[256,8]{0,1:T(8,128)S(1)}, f32[256,8]{0,1:T(8,128)}, u32[]{:S(2)}) copy-start(f32[256,8]{0,1:T(8,128)} %param.21) | copy-start | bytes 24580
  114.5 93.4 %all-gather.16.cloned.1.call-start = ((), (), s32[]{:S(2)}) async-start(), calls=%async_computation.7 | async-start | bytes 2359296 | tf_op jit(solution)/shard_map/all_gather | solution.py:103
  115.1 192.3 %reduce-scatter.10.cloned.1.call-start = ((), (), s32[]{:S(2)}) async-start(), calls=%async_computation.10 | async-start | bytes 4325376
  135.6 30.0 %copy-start.5 = (f32[256,256]{1,0:T(8,128)}, f32[256,256]{1,0:T(8,128)S(1)}, u32[]{:S(2)}) copy-start(f32[256,256]{1,0:T(8,128)S(1)} %fusion.57) | copy-start | bytes 786436
  219.2 0.9 copy-start.7
  219.2 89.2 %copy-start.9 = (f32[512]{0:T(512)S(1)}, f32[512]{0:T(512)}, u32[]{:S(2)}) copy-start(f32[512]{0:T(512)} %param.16) | copy-start | bytes 6148
  219.2 145.0 %copy-start.2 = (bf16[256,4096]{1,0:T(8,128)(2,1)S(1)}, bf16[256,4096]{1,0:T(8,128)(2,1)}, u32[]{:S(2)}) copy-start(bf16[256,4096]{1,0:T(8,128)(2,1)} %all-gather.16.cloned.1.call-done) | copy-start | bytes 6291460
  219.2 145.0 %all-gather.14.cloned.1.call-start = ((), (), s32[]{:S(2)}) async-start(), calls=%async_computation.5 | async-start | bytes 4325376 | tf_op jit(solution)/shard_map/all_gather | solution.py:101
  309.3 60.3 %copy-start.6 = (f32[256,256]{1,0:T(8,128)S(1)}, f32[256,256]{1,0:T(8,128)}, u32[]{:S(2)}) copy-start(f32[256,256]{1,0:T(8,128)} %copy-done.5) | copy-start | bytes 786436
  309.3 111.2 %all-gather.20.cloned.1.call-start = ((), (), s32[]{:S(2)}) async-start(), calls=%async_computation.9 | async-start | bytes 4325376 | tf_op jit(solution)/shard_map/all_gather | solution.py:19
  367.6 0.8 copy-start.4
  369.5 191.3 %reduce-scatter.12.cloned.1.call-start = ((), (), s32[]{:S(2)}) async-start(), calls=%async_computation.11 | async-start | bytes 4325376
  428.5 1.6 copy-start.1
  439.9 166.1 %reduce-scatter.8.cloned.1.call-start = ((), (), s32[]{:S(2)}) async-start(), calls=%async_computation.6 | async-start | bytes 2359296 | tf_op jit(solution)/shard_map/reduce_scatter | solution.py:164
Sparse Core Ops, SparseCore 0:
  9.8 44.0 all-gather.9
  56.9 52.3 all-gather.11
  114.6 50.8 all-gather.17
  167.2 40.6 all-gather.15
  219.3 88.0 reduce-scatter.9
  310.6 53.5 all-gather.13
  369.6 50.7 all-gather.19
  440.0 120.7 reduce-scatter.11
  563.9 42.0 reduce-scatter.7
where the time goes:
time: 614 us; the launch traced here: 613 us
  waiting for transfers between devices  381 us (62%)
  blocking collectives  120 us (20%)
  local copies, waits for them, and re-layouts  55.6 us (9%)
  matrix products  30.2 us (5%)
  between operations  14.1 us (2%)
  other arithmetic  10.6 us (2%)
    unnamed x11, waiting for transfers between devices  119 us
    psum x1, blocking collectives, per_device(): in_sum = lax.psum(in_part, 'seq')  83.4 us
    all_gather x2, waiting for transfers between devices, prefix(): lax.all_gather(a.astype(kind), axis)  75.5 us
    all_gather x1, waiting for transfers between devices, per_device(): lax.all_gather(out_levels.astype(jnp.bfloat16), 'seq', axis=0, tiled=True)  55.4 us
    all_gather x1, waiting for transfers between devices, per_device(): lax.all_gather(in_levels.astype(jnp.bfloat16), 'seq', axis=0, tiled=True)  54.8 us
    all_gather x1, waiting for transfers between devices, per_device(): cotangent = lax.all_gather(grad_out, 'tp', axis=1, tiled=True)  41.5 us
    dynamic_slice x62, local copies, waits for them, and re-layouts, one(): lax.dynamic_index_in_dim(a, source, 0, False).astype(own.dtype)  34 us
    reduce_scatter x1, waiting for transfers between devices, per_device(): lax.psum_scatter(partial_tokens.astype(jnp.bfloat16), 'tp', scatter_dimen...  25.3 us
  transfers between devices with their start and end apart: 9, of which 9 were waited for; matrix products, arithmetic and copies ran while one was open for 9% of the time, Pallas kernels for 0%

commit v1 on v0

--- a/solution.py
+++ b/solution.py
@@ -167,7 +167,9 @@
     in_part = jnp.sum(in_total * in_slopes, axis=0)
     out_part = jnp.sum(out_total * out_slopes, axis=1)
     in_sum = lax.psum(in_part, "seq")
-    out_sum = lax.psum(out_part, "tp")
+    out_sum = out_part
+    for hop in (1, 2, 4):
+        out_sum = out_sum + lax.ppermute(out_sum, "tp", [(dev, dev ^ hop) for dev in range(8)])
     grad_in_scale = in_sum / jnp.sqrt(jnp.float32(D * QMAX))
     grad_out_scale = out_sum / jnp.sqrt(jnp.float32(HEADS * HEAD_DIM * QMAX))
     return (

time: 614 us -> 646 us (1.052)
  the two profiles are of different devices: /device:TPU:6 before, /device:TPU:1 now
where the time goes in v1:
time: 646 us; the launch traced here: 645 us
  waiting for transfers between devices  439 us (68%)
  blocking collectives  86.3 us (13%)
  local copies, waits for them, and re-layouts  55.6 us (9%)
  matrix products  30.2 us (5%)
  between operations  14.1 us (2%)
  other arithmetic  10.6 us (2%)
  starting transfers between devices  7.72 us (1%)
    unnamed x11, waiting for transfers between devices  209 us
    all_gather x2, waiting for transfers between devices, prefix(): lax.all_gather(a.astype(kind), axis)  73.6 us
    psum x1, blocking collectives, per_device(): in_sum = lax.psum(in_part, 'seq')  65.8 us
    all_gather x1, waiting for transfers between devices, per_device(): lax.all_gather(out_levels.astype(jnp.bfloat16), 'seq', axis=0, tiled=True)  60 us
    all_gather x1, waiting for transfers between devices, per_device(): lax.all_gather(in_levels.astype(jnp.bfloat16), 'seq', axis=0, tiled=True)  57 us
    all_gather x1, waiting for transfers between devices, per_device(): cotangent = lax.all_gather(grad_out, 'tp', axis=1, tiled=True)  38.7 us
    dynamic_slice x62, local copies, waits for them, and re-layouts, one(): lax.dynamic_index_in_dim(a, source, 0, False).astype(own.dtype)  34 us
    all_gather x1, blocking collectives, prefix(): lax.all_gather(a.astype(kind), axis)  20.6 us
  transfers between devices with their start and end apart: 12, of which 9 were waited for; matrix products, arithmetic and copies ran while one was open for 9% of the time, Pallas kernels for 0%

profile of v1, /device:TPU:1, one launch (start us, length us, event | category | flops | bytes accessed | tf_op | source)
XLA Modules:
  0.0 645.2 jit_solution(15842385427275647314)
XLA Ops:
  8.0 1.0 copy.60
  10.5 1.3 reduce-window.14
  12.4 38.7 %all-gather.10.cloned.1.call-done = bf16[256,4096]{1,0:T(8,128)(2,1)} async-done(((bf16[256,512]{1,0:T(8,128)(2,1)}), bf16[256,4096]{1,0:T(8,128)(2,1)}) %all-gather.10.cloned.1.call-update) | async-done | bytes 2097168 | tf_op jit(solution)/shard_map/all_gather | solution.py:104
  51.1 60.0 %all-gather.12.cloned.1.call-done = bf16[4096,512]{0,1:T(8,128)(2,1)} async-done(((bf16[128,512]{0,1:T(8,128)(2,1)}), bf16[4096,512]{0,1:T(8,128)(2,1)}) %all-gather.12.cloned.1.call-update) | async-done | bytes 4194320 | tf_op jit(solution)/shard_map/all_gather | solution.py:102
  111.1 4.1 fusion.2
  115.2 1.1 fusion.20
  118.0 20.6 %all-gather.2 = bf16[32,1,8]{2,1,0:T(2,128)(2,1)S(1)} all-gather(bf16[1,1,8]{2,1,0:T(2,128)(2,1)S(1)} %bitcast.154), channel_id=1, replica_groups=mesh['seq'=32,'tp'=8] {'seq'}, dimensions={0}, use_global_device_ids=true | all-gather | bytes 528 | tf_op jit(solution)/shard_map/all_gather | solution.py:19
  139.0 1.8 fusion.6
  140.9 26.3 %all-gather.18.cloned.1.call-done = bf16[256,128,64]{1,2,0:T(8,128)(2,1)} async-done(((bf16[8,128,64]{1,2,0:T(8,128)(2,1)}), bf16[256,128,64]{1,2,0:T(8,128)(2,1)}) %all-gather.18.cloned.1.call-update) | async-done | bytes 4194320 | tf_op jit(solution)/shard_map/all_gather | solution.py:19
  167.2 39.1 %while.16 = (s32[]{:T(128)}, f32[8,128,64]{2,1,0:T(8,128)S(1)}, s32[]{:T(128)}, bf16[32,8,128,64]{2,3,1,0:T(8,128)(2,1)}, bf16[32,8]{1,0:T(8,128)(2,1)S(1)}, /*index=5*/s32[]{:T(128)}, s32[]{:T(128)}, s32[]{:T(128)}, s32[]{:T(128)}) while((s32[]{:T(128)}, f32[8,128,64]{2,1,0:T(8,128)S(1)}, s32[]{:T(128)}, bf16[32,8,128,64]{2,3,1,0:T(8,128)(2,1)}, ...), condition=%wide.region_5.6_spmd, body=%wide.region_4.5_spmd.sunk | while | flops 196622 | bytes 1179883 | solution.py:34
  167.3 0.9 constant_dynamic-slice_fusion.4
  168.6 0.9 constant_dynamic-slice_fusion.4
  169.9 0.9 constant_dynamic-slice_fusion.4
  171.2 0.9 constant_dynamic-slice_fusion.4
  172.5 0.9 constant_dynamic-slice_fusion.4
  173.8 0.9 constant_dynamic-slice_fusion.4
  175.1 0.9 constant_dynamic-slice_fusion.4
  176.4 0.9 constant_dynamic-slice_fusion.4
  177.7 0.9 constant_dynamic-slice_fusion.4
  179.0 0.9 constant_dynamic-slice_fusion.4
  180.3 0.9 constant_dynamic-slice_fusion.4
  181.6 0.9 constant_dynamic-slice_fusion.4
  182.9 0.9 constant_dynamic-slice_fusion.4
  184.2 0.9 constant_dynamic-slice_fusion.4
  185.5 0.9 constant_dynamic-slice_fusion.4
  186.8 0.9 constant_dynamic-slice_fusion.4
  188.1 0.9 constant_dynamic-slice_fusion.4
  189.4 0.9 constant_dynamic-slice_fusion.4
  190.7 0.9 constant_dynamic-slice_fusion.4
  192.0 0.9 constant_dynamic-slice_fusion.4
  193.3 0.9 constant_dynamic-slice_fusion.4
  194.6 0.9 constant_dynamic-slice_fusion.4
  195.9 0.9 constant_dynamic-slice_fusion.4
  197.2 0.9 constant_dynamic-slice_fusion.4
  198.6 0.9 constant_dynamic-slice_fusion.4
  199.9 0.9 constant_dynamic-slice_fusion.4
  201.2 0.9 constant_dynamic-slice_fusion.4
  202.5 0.9 constant_dynamic-slice_fusion.4
  203.8 0.9 constant_dynamic-slice_fusion.4
  205.1 0.9 constant_dynamic-slice_fusion.4
  207.5 4.8 fusion
  212.3 6.5 copy.81
  219.8 87.1 %reduce-scatter.10.cloned.1.call-done = bf16[128,512]{1,0:T(8,128)(2,1)} async-done(((bf16[4096,512]{1,0:T(8,128)(2,1)}), bf16[128,512]{1,0:T(8,128)(2,1)}) %reduce-scatter.10.cloned.1.call-update) | async-done | bytes 131088
  306.9 1.0 copy.82
  307.9 0.9 fusion.34
  308.9 57.0 %all-gather.14.cloned.1.call-done = bf16[4096,512]{0,1:T(8,128)(2,1)} async-done(((bf16[128,512]{0,1:T(8,128)(2,1)}), bf16[4096,512]{0,1:T(8,128)(2,1)}) %all-gather.14.cloned.1.call-update) | async-done | bytes 4194320 | tf_op jit(solution)/shard_map/all_gather | solution.py:101
  365.9 3.5 convolution_multiply_fusion
  370.1 1.0 fusion.19
  371.3 3.5 fusion.7
  374.7 47.3 %all-gather.20.cloned.1.call-done = bf16[256,128,64]{1,2,0:T(8,128)(2,1)} async-done(((bf16[8,128,64]{1,2,0:T(8,128)(2,1)}), bf16[256,128,64]{1,2,0:T(8,128)(2,1)}) %all-gather.20.cloned.1.call-update) | async-done | bytes 4194320 | tf_op jit(solution)/shard_map/all_gather | solution.py:19
  422.1 1.5 while.17
  422.1 0.9 constant_dynamic-slice_fusion.5
  425.2 3.2 fusion.1
  428.4 6.5 %copy.83 = bf16[4096,512]{1,0:T(8,128)(2,1)} copy(bf16[4096,512]{0,1:T(8,128)(2,1)} %fusion.1) | data formatting | bytes 8388608
  435.1 4.8 convolution_convert_fusion.2
  440.0 120.1 %reduce-scatter.12.cloned.1.call-done = bf16[128,512]{1,0:T(8,128)(2,1)} async-done(((bf16[4096,512]{1,0:T(8,128)(2,1)}), bf16[128,512]{1,0:T(8,128)(2,1)}) %reduce-scatter.12.cloned.1.call-update) | async-done | bytes 131088
  560.1 1.0 copy.84
  561.3 1.4 collective-permute-start
  562.7 1.1 collective-permute-done
  563.8 2.3 collective-permute-start.1
  566.0 65.8 %psum.7 = f32[512]{0:T(512)S(1)} all-reduce(f32[512]{0:T(512)S(1)} %get-tuple-element.273), channel_id=1, replica_groups=mesh['seq'=32,'tp'=8] {'seq'}, use_global_device_ids=true, to_apply=%region_9.10 | all-reduce | flops 512 | bytes 4096 | tf_op jit(solution)/shard_map/psum | solution.py:169
  631.8 3.7 collective-permute-start.2
  636.1 0.8 copy.72
  637.0 0.8 copy.73
  (170 shorter events, 22.2 us)
Async XLA Ops:
  7.2 131.7 %copy-start = (bf16[256,128]{1,0:T(8,128)(2,1)S(1)}, bf16[256,128]{1,0:T(8,128)(2,1)}, u32[]{:S(2)}) copy-start(bf16[256,128]{1,0:T(8,128)(2,1)} %param.19) | copy-start | bytes 196612
  7.2 43.9 %all-gather.10.cloned.1.call-start = ((), (), s32[]{:S(2)}) async-start(), calls=%async_computation.3 | async-start | bytes 2359296 | tf_op jit(solution)/shard_map/all_gather | solution.py:104
  7.9 103.2 %all-gather.12.cloned.1.call-start = ((), (), s32[]{:S(2)}) async-start(), calls=%async_computation.4 | async-start | bytes 4325376 | tf_op jit(solution)/shard_map/all_gather | solution.py:102
  10.5 156.7 %all-gather.18.cloned.1.call-start = ((), (), s32[]{:S(2)}) async-start(), calls=%async_computation.8 | async-start | bytes 4325376 | tf_op jit(solution)/shard_map/all_gather | solution.py:19
  12.4 102.8 %copy-start.3 = (bf16[256,128]{1,0:T(8,128)(2,1)S(1)}, bf16[256,128]{1,0:T(8,128)(2,1)}, u32[]{:S(2)}) copy-start(bf16[256,128]{1,0:T(8,128)(2,1)} %param.20) | copy-start | bytes 196612
  12.4 104.5 %copy-start.8 = (f32[256,8]{0,1:T(8,128)S(1)}, f32[256,8]{0,1:T(8,128)}, u32[]{:S(2)}) copy-start(f32[256,8]{0,1:T(8,128)} %param.21) | copy-start | bytes 24580
  116.3 91.2 %all-gather.16.cloned.1.call-start = ((), (), s32[]{:S(2)}) async-start(), calls=%async_computation.7 | async-start | bytes 2359296 | tf_op jit(solution)/shard_map/all_gather | solution.py:103
  116.9 190.0 %reduce-scatter.10.cloned.1.call-start = ((), (), s32[]{:S(2)}) async-start(), calls=%async_computation.10 | async-start | bytes 4325376
  139.0 28.2 %copy-start.5 = (f32[256,256]{1,0:T(8,128)}, f32[256,256]{1,0:T(8,128)S(1)}, u32[]{:S(2)}) copy-start(f32[256,256]{1,0:T(8,128)S(1)} %fusion.57) | copy-start | bytes 786436
  218.7 0.9 copy-start.7
  218.8 89.2 %copy-start.9 = (f32[512]{0:T(512)S(1)}, f32[512]{0:T(512)}, u32[]{:S(2)}) copy-start(f32[512]{0:T(512)} %param.16) | copy-start | bytes 6148
  218.8 147.1 %copy-start.2 = (bf16[256,4096]{1,0:T(8,128)(2,1)S(1)}, bf16[256,4096]{1,0:T(8,128)(2,1)}, u32[]{:S(2)}) copy-start(bf16[256,4096]{1,0:T(8,128)(2,1)} %all-gather.16.cloned.1.call-done) | copy-start | bytes 6291460
  218.8 147.1 %all-gather.14.cloned.1.call-start = ((), (), s32[]{:S(2)}) async-start(), calls=%async_computation.5 | async-start | bytes 4325376 | tf_op jit(solution)/shard_map/all_gather | solution.py:101
  308.8 62.5 %copy-start.6 = (f32[256,256]{1,0:T(8,128)S(1)}, f32[256,256]{1,0:T(8,128)}, u32[]{:S(2)}) copy-start(f32[256,256]{1,0:T(8,128)} %copy-done.5) | copy-start | bytes 786436
  308.8 113.2 %all-gather.20.cloned.1.call-start = ((), (), s32[]{:S(2)}) async-start(), calls=%async_computation.9 | async-start | bytes 4325376 | tf_op jit(solution)/shard_map/all_gather | solution.py:19
  369.3 0.8 copy-start.4
  371.2 188.9 %reduce-scatter.12.cloned.1.call-start = ((), (), s32[]{:S(2)}) async-start(), calls=%async_computation.11 | async-start | bytes 4325376
  423.6 1.6 copy-start.1
  435.0 203.8 %reduce-scatter.8.cloned.1.call-start = ((), (), s32[]{:S(2)}) async-start(), calls=%async_computation.6 | async-start | bytes 2359296 | tf_op jit(solution)/shard_map/reduce_scatter | solution.py:164
  561.3 2.5 collective-permute-start
  563.8 68.0 %collective-permute-start.1 = (f32[128]{0:T(128)S(1)}, f32[128]{0:T(128)S(1)}, u32[]{:S(2)}, u32[]{:S(2)}) collective-permute-start(f32[128]{0:T(128)S(1)} %add.102), channel_id=1, source_target_pairs={{0,2},{1,3},{2,0},{3,1},{4,6},{5,7},{6,4},{7,5},{8,10},{9,11},{10,... | collective-permute-start | bytes 1544 | tf_op jit(solution)/shard_map/ppermute | solution.py:172
  631.8 6.4 collective-permute-start.2
Sparse Core Ops, SparseCore 0:
  9.8 41.2 all-gather.9
  54.1 56.9 all-gather.11
  116.4 50.7 all-gather.17
  168.8 36.9 all-gather.15
  218.9 87.9 reduce-scatter.9
  310.1 55.6 all-gather.13
  371.3 50.6 all-gather.19
  435.1 125.0 reduce-scatter.11
  563.3 38.8 reduce-scatter.7
